TPU v7x, 32 devices: a whole 2x2x4 slice. The times are simulated.
32 devices in a mesh: dp: 2 (over x), fsdp: 16 (over z, y, core).
Axes of the slice: x: 2, y: 2, z: 4, core: 2. Of those that a mesh axis runs over, the one named last changes fastest.
Arguments:
- tokens: bfloat16 [18432, 768], P(('dp', 'fsdp')), may hold values from -6 to 6
- gain_attn: bfloat16 [768], P(('dp', 'fsdp')), may hold values from 0.25 to 1.75
- w_qkv: bfloat16 [768, 2304], P(('dp', 'fsdp')), may hold values from -0.21875 to 0.21875
- w_proj: bfloat16 [768, 768], P(('dp', 'fsdp')), may hold values from -2.5 to 2.5
- gain_moe: bfloat16 [768], P(('dp', 'fsdp')), may hold values from 0.25 to 1.75
- w_router: bfloat16 [768, 8], P(('dp', 'fsdp')), may hold values from -0.15625 to 0.15625
- w_in: bfloat16 [8, 768, 3072], P('dp', 'fsdp'), may hold values from -0.21875 to 0.21875
- w_out: bfloat16 [8, 3072, 768], P('dp', 'fsdp'), may hold values from -0.875 to 0.875
- routes: int32 [18432, 2], P(('dp', 'fsdp')), may hold values from 0 to 7, as said below
- slot_ids: int32 [18432, 2], P(('dp', 'fsdp')), may hold values from 0 to 152, as said below
- cotangent: bfloat16 [18432, 768], P(('dp', 'fsdp')), may hold values from -6 to 6
Outputs:
- output: bfloat16 [18432, 768], P(('dp', 'fsdp'))
- grad_tokens: float32 [18432, 768], P(('dp', 'fsdp'))
- d_gain_attn: float32 [768], P(('dp', 'fsdp'))
- d_qkv: float32 [768, 2304], P(('dp', 'fsdp'))
- d_proj: float32 [768, 768], P(('dp', 'fsdp'))
- d_gain_moe: float32 [768], P(('dp', 'fsdp'))
- d_router: float32 [768, 8], P(('dp', 'fsdp'))
- d_in: float32 [8, 768, 3072], P('dp', 'fsdp')
- d_out: float32 [8, 3072, 768], P('dp', 'fsdp')
Inputs may be any that keep to these rules, and one draw needn't show every extreme that they name: `routes`: each row names two different experts. `slot_ids`: among the 576 patches of one device, the pairs routed to one expert hold the distinct slots 0, 1, 2, ... in some priority order; a pair beyond the 152 slots holds 152 and is dropped. On every device some expert gets more than 152 pairs.
All inputs are finite; a program needn't handle non-finite values.
Results may differ from a plain program's by a relative error of at most 0.017.
Values may be sent and summed in bfloat16 or wider, within the bound.
No kernel may reach another device: no remote copies, remote signals or barrier semaphores. Data moves between devices by JAX's collectives and lax.ppermute only.
A program may use at most 320 MiB of HBM per device.

v0:
```python
import jax
import jax.numpy as jnp
from jax import lax
from jax.sharding import PartitionSpec as P

HEADS = 12
HEAD_DIM = 64
EXPERTS = 8
SEQ = 576
CAP = 152
norm_epsilon = 1e-06


def norm_parts(values):
    centre = values - jnp.mean(values, axis=-1, keepdims=True)
    inverse = lax.rsqrt(jnp.mean(centre * centre, axis=-1, keepdims=True) + norm_epsilon)
    return (centre * inverse, inverse)


def norm_back(grad_normed, normed, inverse):
    mean_grad = jnp.mean(grad_normed, axis=-1, keepdims=True)
    mean_cross = jnp.mean(grad_normed * normed, axis=-1, keepdims=True)
    return (grad_normed - mean_grad - normed * mean_cross) * inverse


def gelu_tanh(values):
    return jax.nn.gelu(values, approximate=True)


def head_forward(operands):
    queries, keys_head, values_head = operands
    scores = jnp.einsum(
        "isd,itd->ist", queries, keys_head, preferred_element_type=jnp.float32
    ) * HEAD_DIM ** (-0.5)
    largest = jnp.max(scores, axis=-1, keepdims=True)
    powers = jnp.exp(scores - largest)
    totals = jnp.sum(powers, axis=-1, keepdims=True)
    attn_probs = (powers / totals).astype(jnp.bfloat16)
    head_out = jnp.einsum(
        "ist,itd->isd", attn_probs, values_head, preferred_element_type=jnp.float32
    )
    return (head_out.astype(jnp.bfloat16), (largest + jnp.log(totals))[..., 0])


def head_backward(operands):
    queries, keys_head, values_head, grad_head, log_total = operands
    scores = jnp.einsum(
        "isd,itd->ist", queries, keys_head, preferred_element_type=jnp.float32
    ) * HEAD_DIM ** (-0.5)
    attn_probs = jnp.exp(scores - log_total[..., None])
    grad_probs = jnp.einsum(
        "isd,itd->ist", grad_head, values_head, preferred_element_type=jnp.float32
    )
    row_terms = jnp.sum(attn_probs * grad_probs, axis=-1, keepdims=True)
    grad_scores = (attn_probs * (grad_probs - row_terms)).astype(jnp.bfloat16)
    grad_query = jnp.einsum(
        "ist,itd->isd", grad_scores, keys_head, preferred_element_type=jnp.float32
    ) * HEAD_DIM ** (-0.5)
    grad_key = jnp.einsum(
        "ist,isd->itd", grad_scores, queries, preferred_element_type=jnp.float32
    ) * HEAD_DIM ** (-0.5)
    grad_value = jnp.einsum(
        "ist,isd->itd",
        attn_probs.astype(jnp.bfloat16),
        grad_head,
        preferred_element_type=jnp.float32,
    )
    return (grad_query, grad_key, grad_value)


def expert_forward(expert_rows, w_up, w_down):
    pre_act = jnp.einsum("ecd,edf->ecf", expert_rows, w_up, preferred_element_type=jnp.float32)
    hidden = gelu_tanh(pre_act).astype(jnp.bfloat16)
    result = jnp.einsum("ecf,efd->ecd", hidden, w_down, preferred_element_type=jnp.float32).astype(
        jnp.bfloat16
    )
    return (pre_act, hidden, result)


def expert_backward(expert_rows, pre_act, hidden, grad_result, w_up, w_down):
    grad_hidden = jnp.einsum(
        "ecd,efd->ecf", grad_result, w_down, preferred_element_type=jnp.float32
    )
    ignored, pull_back = jax.vjp(gelu_tanh, pre_act)
    grad_pre = pull_back(grad_hidden)[0].astype(jnp.bfloat16)
    grad_down = jnp.einsum("ecf,ecd->efd", hidden, grad_result, preferred_element_type=jnp.float32)
    grad_up = jnp.einsum("ecd,ecf->edf", expert_rows, grad_pre, preferred_element_type=jnp.float32)
    grad_rows = jnp.einsum(
        "ecf,edf->ecd", grad_pre, w_up, preferred_element_type=jnp.float32
    ).astype(jnp.bfloat16)
    return (grad_up, grad_down, grad_rows)


def gather_dense(gain_attn, w_qkv, w_proj, gain_moe, w_router):
    return (
        lax.all_gather(gain_attn, ("dp", "fsdp"), axis=0, tiled=True),
        lax.all_gather(w_qkv, ("dp", "fsdp"), axis=0, tiled=True),
        lax.all_gather(w_proj, ("dp", "fsdp"), axis=0, tiled=True),
        lax.all_gather(gain_moe, ("dp", "fsdp"), axis=0, tiled=True),
        lax.all_gather(w_router, ("dp", "fsdp"), axis=0, tiled=True),
    )


def gather_experts(w_in, w_out):
    local_pair = (w_in, w_out)
    return (
        lax.all_gather(local_pair[0], "fsdp", axis=1, tiled=True),
        lax.all_gather(local_pair[1], "fsdp", axis=1, tiled=True),
    )


def reduce_experts(grad_up, grad_down):
    reduced = (
        lax.psum_scatter(
            grad_up.astype(jnp.bfloat16), "fsdp", scatter_dimension=1, tiled=True
        ).astype(jnp.float32),
        lax.psum_scatter(
            grad_down.astype(jnp.bfloat16), "fsdp", scatter_dimension=1, tiled=True
        ).astype(jnp.float32),
    )
    return reduced


def per_device(
    tokens, gain_attn, w_qkv, w_proj, gain_moe, w_router, w_in, w_out, routes, slot_ids, cotangent
):
    dense_full = gather_dense(gain_attn, w_qkv, w_proj, gain_moe, w_router)
    expert_weights = gather_experts(w_in, w_out)
    rows_here = tokens.shape[0]
    images = rows_here // SEQ
    residual = tokens.astype(jnp.float32)
    normed_one, inverse_one = norm_parts(residual)
    gain_one = dense_full[0].astype(jnp.float32)
    act_one = (normed_one * gain_one).astype(jnp.bfloat16)
    qkv = jnp.dot(act_one, dense_full[1], preferred_element_type=jnp.float32).astype(jnp.bfloat16)
    split_qkv = qkv.reshape(images, SEQ, 3, HEADS, HEAD_DIM).transpose(2, 3, 0, 1, 4)
    head_out, head_lse = lax.map(head_forward, (split_qkv[0], split_qkv[1], split_qkv[2]))
    attended = head_out.transpose(1, 2, 0, 3).reshape(rows_here, -1)
    resid_mid = residual + jnp.dot(attended, dense_full[2], preferred_element_type=jnp.float32)
    normed_two, inverse_two = norm_parts(resid_mid)
    gain_two = dense_full[3].astype(jnp.float32)
    act_two = (normed_two * gain_two).astype(jnp.bfloat16)
    logits = jnp.dot(act_two, dense_full[4], preferred_element_type=jnp.float32)
    router = jax.nn.softmax(logits, axis=-1)
    expert_ids = lax.broadcasted_iota(jnp.int32, (1, 1, EXPERTS), 2)
    chosen = routes[:, :, None] == expert_ids
    gate_values = jnp.sum(jnp.where(chosen, router[:, None, :], 0.0), axis=-1)
    gates_low = gate_values.astype(jnp.bfloat16)
    slot_count = EXPERTS * CAP
    columns = lax.broadcasted_iota(jnp.int32, (1, 1, slot_count), 2)
    live_pair = slot_ids < CAP
    targets = routes * CAP + slot_ids
    matches = (targets[:, :, None] == columns) & live_pair[:, :, None]
    dispatch = jnp.sum(matches.astype(jnp.bfloat16), axis=1)
    combine = jnp.sum(
        jnp.where(matches, gates_low[:, :, None], jnp.zeros((), jnp.bfloat16)), axis=1
    )
    slot_rows = (
        jnp.einsum("tx,td->xd", dispatch, act_two, preferred_element_type=jnp.float32)
        .astype(jnp.bfloat16)
        .reshape(EXPERTS, CAP, -1)
    )
    expert_rows = lax.all_to_all(slot_rows, "dp", split_axis=0, concat_axis=1, tiled=True)
    pre_act, hidden, result = expert_forward(expert_rows, expert_weights[0], expert_weights[1])
    slot_result = lax.all_to_all(result, "dp", split_axis=1, concat_axis=0, tiled=True)
    flat_result = slot_result.reshape(slot_count, -1)
    moe_sum = jnp.einsum("tx,xd->td", combine, flat_result, preferred_element_type=jnp.float32)
    output = (resid_mid + moe_sum).astype(jnp.bfloat16)
    dense_full = gather_dense(gain_attn, w_qkv, w_proj, gain_moe, w_router)
    expert_weights = gather_experts(w_in, w_out)
    grad_slots = (
        jnp.einsum("tx,td->xd", combine, cotangent, preferred_element_type=jnp.float32)
        .astype(jnp.bfloat16)
        .reshape(EXPERTS, CAP, -1)
    )
    picked = flat_result[jnp.clip(targets, 0, slot_count - 1)]
    grad_gates = jnp.where(
        live_pair,
        jnp.einsum("tkd,td->tk", picked, cotangent, preferred_element_type=jnp.float32),
        0.0,
    )
    grad_router = jnp.sum(jnp.where(chosen, grad_gates[:, :, None], 0.0), axis=1)
    grad_logits = (
        router * (grad_router - jnp.sum(router * grad_router, axis=-1, keepdims=True))
    ).astype(jnp.bfloat16)
    d_router = jnp.einsum("td,te->de", act_two, grad_logits, preferred_element_type=jnp.float32)
    grad_act_two = jnp.einsum(
        "te,de->td", grad_logits, dense_full[4], preferred_element_type=jnp.float32
    )
    grad_expert = lax.all_to_all(grad_slots, "dp", split_axis=0, concat_axis=1, tiled=True)
    grad_up, grad_down, grad_rows = expert_backward(
        expert_rows, pre_act, hidden, grad_expert, expert_weights[0], expert_weights[1]
    )
    grad_rows = lax.all_to_all(grad_rows, "dp", split_axis=1, concat_axis=0, tiled=True)
    grad_act_two = grad_act_two + jnp.einsum(
        "tx,xd->td", dispatch, grad_rows.reshape(slot_count, -1), preferred_element_type=jnp.float32
    )
    d_gain_moe = jnp.sum(grad_act_two * normed_two, axis=0)
    grad_mid = cotangent.astype(jnp.float32) + norm_back(
        grad_act_two * gain_two, normed_two, inverse_two
    )
    grad_mid_low = grad_mid.astype(jnp.bfloat16)
    d_proj = jnp.einsum("td,te->de", attended, grad_mid_low, preferred_element_type=jnp.float32)
    grad_attended = jnp.einsum(
        "te,de->td", grad_mid_low, dense_full[2], preferred_element_type=jnp.float32
    ).astype(jnp.bfloat16)
    grad_heads = grad_attended.reshape(images, SEQ, HEADS, HEAD_DIM).transpose(2, 0, 1, 3)
    grad_query, grad_key, grad_value = lax.map(
        head_backward, (split_qkv[0], split_qkv[1], split_qkv[2], grad_heads, head_lse)
    )
    grad_qkv = (
        jnp.stack([grad_query, grad_key, grad_value])
        .transpose(2, 3, 0, 1, 4)
        .reshape(rows_here, -1)
        .astype(jnp.bfloat16)
    )
    d_qkv = jnp.einsum("td,te->de", act_one, grad_qkv, preferred_element_type=jnp.float32)
    grad_act_one = jnp.einsum(
        "te,de->td", grad_qkv, dense_full[1], preferred_element_type=jnp.float32
    )
    d_gain_attn = jnp.sum(grad_act_one * normed_one, axis=0)
    grad_tokens = grad_mid + norm_back(grad_act_one * gain_one, normed_one, inverse_one)
    dense_grads = (
        lax.psum_scatter(d_gain_attn, ("dp", "fsdp"), scatter_dimension=0, tiled=True),
        lax.psum_scatter(d_qkv, ("dp", "fsdp"), scatter_dimension=0, tiled=True),
        lax.psum_scatter(d_proj, ("dp", "fsdp"), scatter_dimension=0, tiled=True),
        lax.psum_scatter(d_gain_moe, ("dp", "fsdp"), scatter_dimension=0, tiled=True),
        lax.psum_scatter(d_router, ("dp", "fsdp"), scatter_dimension=0, tiled=True),
    )
    expert_grads = reduce_experts(grad_up, grad_down)
    return (
        output,
        grad_tokens,
        dense_grads[0],
        dense_grads[1],
        dense_grads[2],
        dense_grads[3],
        dense_grads[4],
        expert_grads[0],
        expert_grads[1],
    )


def solution(mesh):
    in_specs = (
        P(("dp", "fsdp"), None),
        P(("dp", "fsdp")),
        P(("dp", "fsdp"), None),
        P(("dp", "fsdp"), None),
        P(("dp", "fsdp")),
        P(("dp", "fsdp"), None),
        P("dp", "fsdp", None),
        P("dp", "fsdp", None),
        P(("dp", "fsdp"), None),
        P(("dp", "fsdp"), None),
        P(("dp", "fsdp"), None),
    )
    out_specs = (
        P(("dp", "fsdp"), None),
        P(("dp", "fsdp"), None),
        P(("dp", "fsdp")),
        P(("dp", "fsdp"), None),
        P(("dp", "fsdp"), None),
        P(("dp", "fsdp")),
        P(("dp", "fsdp"), None),
        P("dp", "fsdp", None),
        P("dp", "fsdp", None),
    )
    return jax.shard_map(
        per_device, mesh=mesh, in_specs=in_specs, out_specs=out_specs, check_vma=False
    )
```

profile of v0, /device:TPU:0, one launch (start us, length us, event | category | flops | bytes accessed | tf_op | source)
XLA Modules:
  0.0 1001.7 jit_solution(7998535637937780949)
XLA Ops:
  10.6 42.0 %all-reduce.6 = (bf16[768]{0:T(1024)(128)(2,1)S(1)}, bf16[768]{0:T(1024)(128)(2,1)S(1)}) all-reduce(bf16[768]{0:T(1024)(128)(2,1)S(1)} %dynamic-update-slice, bf16[768]{0:T(1024)(128)(2,1)S(1)} %dynamic-update-slice.1), channel_id=1, replica_groups=mesh['dp'=2,'fsdp'=16] {'dp','fsdp'}, use_global_device_ids=true, to_apply=%add | all-reduce | flops 1536 | bytes 6144
  52.6 40.8 %all-gather = bf16[32,24,8]{1,2,0:T(8,128)(2,1)S(1)} all-gather(bf16[1,24,8]{1,2,0:T(8,128)(2,1)S(1)} %bitcast.199), channel_id=1, replica_groups=mesh['dp'=2,'fsdp'=16] {'dp','fsdp'}, dimensions={0}, use_global_device_ids=true | all-gather | bytes 12672 | tf_op jit(solution)/shard_map/all_gather | solution.py:100
  95.4 5.9 convolution_convert_fusion.3
  101.3 4.0 copy.102
  110.8 2.6 copy.105
  113.4 37.9 %while.26 = (s32[]{:T(128)}, bf16[12,1,576,64]{2,3,1,0:T(8,128)(2,1)}, f32[12,1,576]{2,1,0:T(1,128)}, bf16[12,1,576,64]{3,2,1,0:T(8,128)(2,1)S(1)}, bf16[12,1,57...) while((s32[]{:T(128)}, bf16[12,1,576,64]{2,3,1,0:T(8,128)(2,1)}, ...), condition=%wide.region_5.6_spmd, body=%wide.region_2.5_spmd.sunk | while | flops 87293376 | bytes 4531033 | solution.py:137
  114.0 1.9 fusion.134
  117.1 1.9 fusion.134
  120.3 1.9 fusion.134
  123.4 1.9 fusion.134
  126.6 1.9 fusion.134
  129.7 1.9 fusion.134
  132.8 1.9 fusion.134
  136.0 2.0 fusion.134
  139.2 1.9 fusion.134
  142.3 2.0 fusion.134
  145.5 2.0 fusion.134
  148.7 2.0 fusion.134
  151.3 4.1 fusion.75
  157.2 3.7 fusion.48
  160.9 2.9 convolution_convert_fusion.4
  163.8 3.7 all-to-all-start.2
  167.5 4.4 convolution_convert_fusion.5
  171.9 18.5 %all-to-all-done.2 = bf16[8,152,768]{2,1,0:T(8,128)(2,1)S(1)} async-done(((bf16[8,152,768]{2,1,0:T(8,128)(2,1)}), bf16[8,152,768]{2,1,0:T(8,128)(2,1)S(1)}, u32[]{:S(2)}, u32[]{:S(2)}) %all-to-all-start.2) | async-done | bytes 1867808 | tf_op jit(solution)/shard_map/all_to_all | solution.py:190
  191.7 4.8 all-to-all-start
  198.6 20.2 %all-to-all-done = bf16[8,152,768]{2,1,0:T(8,128)(2,1)} async-done(((bf16[8,152,768]{2,1,0:T(8,128)(2,1)}), bf16[8,152,768]{2,1,0:T(8,128)(2,1)}, u32[]{:S(2)}, u32[]{:S(2)}) %all-to-all-start) | async-done | bytes 1867808 | tf_op jit(solution)/shard_map/all_to_all | solution.py:163
  218.8 2.9 copy.107
  221.7 7.1 all-gather.12.cloned.1.call-done
  228.8 12.9 %fusion.77 = f32[4,304,3072]{2,1,0:T(8,128)} fusion(bf16[4,304,768]{2,1,0:T(8,128)(2,1)S(1)} %bitcast.182, bf16[4,3072,768]{2,1,0:T(8,128)(2,1)} %all-gather.12.cloned.1.call-done), kind=kOutput, calls=%fused_computation.141 | convolution fusion | flops 5737807872 | bytes 35684352 | tf_op jit(solution)/shard_map/ecd,efd->ecf/dot_general | solution.py:81
  241.7 87.4 %all-gather.10.cloned.1.call-done = bf16[4,768,3072]{2,1,0:T(8,128)(2,1)} async-done(((bf16[4,48,3072]{2,1,0:T(8,128)(2,1)}), bf16[4,768,3072]{2,1,0:T(8,128)(2,1)}) %all-gather.10.cloned.1.call-update) | async-done | bytes 18874384 | tf_op jit(solution)/shard_map/all_gather | solution.py:107
  329.1 26.9 %fusion.43 = (bf16[4,304,3072]{2,1,0:T(8,128)(2,1)}, f32[4,304,3072]{2,1,0:T(8,128)}) fusion(f32[4,304,3072]{2,1,0:T(8,128)} %fusion.77, bf16[4,304,768]{2,1,0:T(8,128)(2,1)} %bitcast.192, bf16[4,768,3072]{2,1,0:T(8,128)(2,1)} %all-gather.10.cloned.1.call-done), kind=kOutput, calls=%fused_computation.59 | convolution fusion | flops 5812518912 | bytes 58097664 | tf_op jit(solution)/shard_map/ecd,edf->ecf/dot_general | solution.py:72
  356.0 16.5 %convolution_convert_fusion.2 = bf16[4,768,3072]{2,1,0:T(8,128)(2,1)} fusion(bf16[4,304,768]{2,1,0:T(8,128)(2,1)} %bitcast.193, bf16[4,304,3072]{2,1,0:T(8,128)(2,1)} %get-tuple-element.212), kind=kOutput, calls=%fused_computation.62 | convolution fusion | flops 5747245056 | bytes 28213248 | tf_op jit(solution)/shard_map/ecd,ecf->edf/dot_general | solution.py:87
  372.8 20.0 %convolution_convert_fusion.1 = bf16[4,3072,768]{2,1,0:T(8,128)(2,1)} fusion(bf16[4,304,768]{2,1,0:T(8,128)(2,1)S(1)} %bitcast.183, f32[4,304,3072]{2,1,0:T(8,128)} %get-tuple-element.213), kind=kOutput, calls=%fused_computation.61 | convolution fusion | flops 5780865024 | bytes 35684352 | tf_op jit(solution)/shard_map/ecf,ecd->efd/dot_general | solution.py:86
  392.9 19.3 %convolution_convert_fusion.7 = bf16[4,304,768]{2,1,0:T(8,128)(2,1)S(1)} fusion(bf16[4,3072,768]{2,1,0:T(8,128)(2,1)} %all-gather.12.cloned.1.call-done, f32[4,304,3072]{2,1,0:T(8,128)} %get-tuple-element.213), kind=kOutput, calls=%fused_computation.85 | convolution fusion | flops 5772361728 | bytes 35684352 | tf_op jit(solution)/shard_map/ecf,efd->ecd/dot_general | solution.py:74
  412.2 2.2 copy.108
  414.4 3.9 all-to-all-start.1
  418.4 13.2 %convolution_convert_fusion.6 = bf16[4,304,768]{2,1,0:T(8,128)(2,1)} fusion(bf16[4,304,3072]{2,1,0:T(8,128)(2,1)} %get-tuple-element.212, bf16[4,768,3072]{2,1,0:T(8,128)(2,1)} %all-gather.10.cloned.1.call-done), kind=kOutput, calls=%fused_computation.84 | convolution fusion | flops 5738741760 | bytes 28213248 | tf_op jit(solution)/shard_map/ecf,edf->ecd/dot_general | solution.py:88
  431.6 3.7 copy.112
  435.3 6.1 all-to-all-done.1
  442.6 4.8 all-to-all-start.3
  449.7 20.1 %all-to-all-done.3 = bf16[4,304,768]{2,0,1:T(4,128)(2,1)} async-done(((bf16[4,304,768]{2,0,1:T(4,128)(2,1)}), bf16[4,304,768]{2,0,1:T(4,128)(2,1)}, u32[]{:S(2)}, u32[]{:S(2)}) %all-to-all-start.3) | async-done | bytes 1867808 | tf_op jit(solution)/shard_map/all_to_all | solution.py:194
  472.9 4.8 gather_fusion
  477.7 4.7 reshape.217
  482.4 6.0 fusion.62
  489.7 3.0 fusion.78
  499.1 4.3 fusion.66
  503.7 100.7 %while.27 = (s32[]{:T(128)}, bf16[12,1,576,64]{2,3,1,0:T(8,128)(2,1)}, bf16[12,1,576,64]{2,3,1,0:T(8,128)(2,1)}, bf16[12,1,576,64]{2,3,1,0:T(8,128)(2,1)}, bf16[...) while((s32[]{:T(128)}, ...), condition=%wide.region_19.20_spmd, body=%wide.region_17.19_spmd.sunk | while | flops 215064000 | bytes 11510129 | solution.py:208
  524.0 1.9 fusion.144
  534.2 1.9 fusion.145
  550.9 1.9 fusion.145
  575.9 1.9 fusion.145
  584.4 2.0 fusion.145
  593.0 1.9 fusion.145
  601.5 1.9 fusion.145
  608.4 5.5 fusion.71
  615.2 7.2 fusion.60
  622.4 43.2 %all-reduce.5 = (f32[768]{0:T(1024)S(1)}, f32[768]{0:T(1024)S(1)}, f32[768,8]{0,1:T(8,128)S(1)}) all-reduce(f32[768]{0:T(1024)S(1)} %get-tuple-element.158, f32[768]{0:T(1024)S(1)} %get-tuple-element.156, f32[768,8]{0,1:T(8,128)S(1)} %fusion.79), channel_id=2, replica_groups=mesh['dp'=2,'fsdp'=16] {'dp','fsdp'}, use_global_device_ids=true, to_apply=%region_23.24.clone | all-reduce | flops 7680 | bytes 61440
  667.4 4.0 fusion.59
  671.4 2.2 add_convert_fusion
  673.7 3.0 convert_element_type.122
  676.7 88.2 %reduce-scatter.12.cloned.1.call-done = bf16[4,192,768]{2,1,0:T(8,128)(2,1)} async-done(((bf16[4,3072,768]{2,1,0:T(8,128)(2,1)}), bf16[4,192,768]{2,1,0:T(8,128)(2,1)}) %reduce-scatter.12.cloned.1.call-update) | async-done | bytes 1179664 | tf_op jit(solution)/shard_map/reduce_scatter | solution.py:117
  764.9 2.9 convert_element_type.124
  767.8 101.8 %reduce-scatter.8.cloned.1.call-done = f32[24,768]{1,0:T(8,128)} async-done(((f32[768,768]{1,0:T(8,128)}), f32[24,768]{1,0:T(8,128)}) %reduce-scatter.8.cloned.1.call-update) | async-done | bytes 73744 | tf_op jit(solution)/shard_map/reduce_scatter | solution.py:226
  869.6 124.8 %reduce-scatter.6.cloned.1.call-done = f32[24,2304]{1,0:T(8,128)} async-done(((f32[768,2304]{1,0:T(8,128)}), f32[24,2304]{1,0:T(8,128)}) %reduce-scatter.6.cloned.1.call-update) | async-done | bytes 221200 | tf_op jit(solution)/shard_map/reduce_scatter | solution.py:225
  (276 shorter events, 138.9 us)
Async XLA Ops:
  7.2 2.9 copy-start.36
  7.2 3.1 copy-start.37
  7.2 45.4 %copy-start.34 = (bf16[24,8]{0,1:T(8,128)(2,1)S(1)}, bf16[24,8]{0,1:T(8,128)(2,1)}, u32[]{:S(2)}) copy-start(bf16[24,8]{0,1:T(8,128)(2,1)} %param.20) | copy-start | bytes 1156
  7.2 86.3 %copy-start.8 = (bf16[576,768]{1,0:T(8,128)(2,1)S(1)}, bf16[576,768]{1,0:T(8,128)(2,1)}, u32[]{:S(2)}) copy-start(bf16[576,768]{1,0:T(8,128)(2,1)} %param.15) | copy-start | bytes 2654212
  7.2 88.2 %all-gather.6.cloned.1.call-start = ((), (), s32[]{:S(2)}) async-start(), calls=%async_computation.8 | async-start | bytes 3649536 | tf_op jit(solution)/shard_map/all_gather | solution.py:97
  8.0 143.4 %all-gather.8.cloned.1.call-start = ((), (), s32[]{:S(2)}) async-start(), calls=%async_computation.9 | async-start | bytes 1216512 | tf_op jit(solution)/shard_map/all_gather | solution.py:98
  8.7 220.1 %all-gather.12.cloned.1.call-start = ((), (), s32[]{:S(2)}) async-start(), calls=%async_computation.11 | async-start | bytes 20054016 | tf_op jit(solution)/shard_map/all_gather | solution.py:108
  9.4 84.7 %copy-start.21 = (s32[576,2]{0,1:T(2,128)S(1)}, s32[576,2]{0,1:T(2,128)}, u32[]{:S(2)}) copy-start(s32[576,2]{0,1:T(2,128)} %param.24) | copy-start | bytes 13828
  9.4 85.3 %copy-start.23 = (s32[576,2]{0,1:T(2,128)S(1)}, s32[576,2]{0,1:T(2,128)}, u32[]{:S(2)}) copy-start(s32[576,2]{0,1:T(2,128)} %param.23) | copy-start | bytes 13828
  9.5 319.6 %all-gather.10.cloned.1.call-start = ((), (), s32[]{:S(2)}) async-start(), calls=%async_computation.10 | async-start | bytes 20054016 | tf_op jit(solution)/shard_map/all_gather | solution.py:107
  52.6 42.8 %copy-start.29 = (f32[768]{0:T(1024)}, f32[768]{0:T(1024)S(1)}, u32[]{:S(2)}) copy-start(f32[768]{0:T(1024)S(1)} %convert_element_type.101) | copy-start | bytes 9220
  93.7 1.6 copy-start.25
  94.8 0.6 copy-start.31
  151.3 4.1 copy-start.4
  151.3 4.2 copy-start.5
  155.5 1.2 copy-start
  155.9 1.2 copy-start.24
  155.9 1.3 copy-start.27
  155.9 1.3 copy-start.33
  156.7 10.9 %copy-start.6 = (bf16[576,768]{1,0:T(8,128)(2,1)}, bf16[576,768]{1,0:T(8,128)(2,1)S(1)}, u32[]{:S(2)}) copy-start(bf16[576,768]{1,0:T(8,128)(2,1)S(1)} %multiply_convert_fusion.2) | copy-start | bytes 2654212
  156.7 4.2 copy-start.19
  160.9 2.9 copy-start.14
  163.8 26.7 %all-to-all-start.2 = ((bf16[8,152,768]{2,1,0:T(8,128)(2,1)}), bf16[8,152,768]{2,1,0:T(8,128)(2,1)S(1)}, u32[]{:S(2)}, u32[]{:S(2)}) async-start(bf16[8,152,768]{2,1,0:T(8,128)(2,1)} %bitcast.194), calls=%async_computation.2 | async-start | bytes 3735552 | tf_op jit(solution)/shard_map/all_to_all | solution.py:190
  190.5 1.2 copy-start.12
  191.7 27.1 %all-to-all-start = ((bf16[8,152,768]{2,1,0:T(8,128)(2,1)}), bf16[8,152,768]{2,1,0:T(8,128)(2,1)}, u32[]{:S(2)}, u32[]{:S(2)}) async-start(bf16[8,152,768]{2,1,0:T(8,128)(2,1)} %bitcast.191), calls=%async_computation | async-start | bytes 3735552 | tf_op jit(solution)/shard_map/all_to_all | solution.py:163
  196.5 477.2 %reduce-scatter.10.cloned.1.call-start = ((), (), s32[]{:S(2)}) async-start(), calls=%async_computation.14 | async-start | bytes 20054016 | tf_op jit(solution)/shard_map/reduce_scatter | solution.py:114
  372.6 392.4 %reduce-scatter.12.cloned.1.call-start = ((), (), s32[]{:S(2)}) async-start(), calls=%async_computation.15 | async-start | bytes 20054016 | tf_op jit(solution)/shard_map/reduce_scatter | solution.py:117
  414.4 27.0 %all-to-all-start.1 = ((bf16[4,304,768]{2,0,1:T(4,128)(2,1)}), bf16[4,304,768]{2,0,1:T(4,128)(2,1)S(1)}, u32[]{:S(2)}, u32[]{:S(2)}) async-start(bf16[4,304,768]{2,0,1:T(4,128)(2,1)} %copy.108), calls=%async_computation.1 | async-start | bytes 3735552 | tf_op jit(solution)/shard_map/all_to_all | solution.py:165
  435.3 12.2 %copy-start.28 = (s32[576,2]{0,1:T(2,128)S(1)}, s32[576,2]{0,1:T(2,128)}, u32[]{:S(2)}) copy-start(s32[576,2]{0,1:T(2,128)} %get-tuple-element.199) | copy-start | bytes 13828
  441.4 1.2 copy-start.11
  442.6 27.1 %all-to-all-start.3 = ((bf16[4,304,768]{2,0,1:T(4,128)(2,1)}), bf16[4,304,768]{2,0,1:T(4,128)(2,1)}, u32[]{:S(2)}, u32[]{:S(2)}) async-start(bf16[4,304,768]{2,0,1:T(4,128)(2,1)} %copy.112), calls=%async_computation.3 | async-start | bytes 3735552 | tf_op jit(solution)/shard_map/all_to_all | solution.py:194
  447.4 422.2 %reduce-scatter.8.cloned.1.call-start = ((), (), s32[]{:S(2)}) async-start(), calls=%async_computation.13 | async-start | bytes 2433024 | tf_op jit(solution)/shard_map/reduce_scatter | solution.py:226
  482.4 7.1 copy-start.22
  482.4 7.3 copy-start.16
  489.7 3.0 copy-start.1
  492.7 1.2 copy-start.20
  493.8 1.9 copy-start.35
  494.5 1.2 copy-start.3
  503.4 491.0 %reduce-scatter.6.cloned.1.call-start = ((), (), s32[]{:S(2)}) async-start(), calls=%async_computation.12 | async-start | bytes 7299072 | tf_op jit(solution)/shard_map/reduce_scatter | solution.py:225
  604.4 1.5 copy-start.17
  604.4 1.8 copy-start.18
  606.1 2.2 copy-start.9
  606.2 2.2 copy-start.26
  606.2 2.2 copy-start.30
  606.2 2.2 copy-start.32
  606.7 1.7 copy-start.13
  613.8 1.2 copy-start.7
  615.2 52.2 %copy-start.10 = (bf16[576,768]{1,0:T(8,128)(2,1)S(1)}, bf16[576,768]{1,0:T(8,128)(2,1)}, u32[]{:S(2)}) copy-start(bf16[576,768]{1,0:T(8,128)(2,1)} %param.15) | copy-start | bytes 2654212
  667.4 4.0 copy-start.2
  667.4 4.0 copy-start.15
Sparse Core Ops, SparseCore 0:
  10.9 62.6 all-gather.5
  76.6 52.6 all-gather.7
  130.9 97.8 all-gather.11
  230.2 98.8 all-gather.9
  372.7 194.0 reduce-scatter.9
  570.7 194.1 reduce-scatter.11
  770.8 98.7 reduce-scatter.7
  875.8 118.5 reduce-scatter.5
where the time goes:
time: 1010 us; the launch traced here: 1000 us
  waiting for transfers between devices  477 us (47%)
  matrix products  276 us (27%)
  blocking collectives  126 us (12%)
  local copies, waits for them, and re-layouts  66.9 us (7%)
  other arithmetic  22.4 us (2%)
  starting transfers between devices  18.3 us (2%)
  between operations  15.1 us (1%)
    reduce_scatter x1, waiting for transfers between devices, per_device(): lax.psum_scatter(d_qkv, ('dp', 'fsdp'), scatter_dimension=0, tiled=True)  125 us
    reduce_scatter x1, waiting for transfers between devices, per_device(): lax.psum_scatter(d_proj, ('dp', 'fsdp'), scatter_dimension=0, tiled=True)  102 us
    reduce_scatter x1, waiting for transfers between devices, reduce_experts(): lax.psum_scatter(grad_down.astype(jnp.bfloat16), 'fsdp', scatter_dimensio...  88.2 us
    all_gather x1, waiting for transfers between devices, gather_experts(): lax.all_gather(local_pair[0], 'fsdp', axis=1, tiled=True)  87.4 us
    unnamed x2, blocking collectives  85.2 us
    all_gather x1, blocking collectives, gather_dense(): lax.all_gather(w_router, ('dp', 'fsdp'), axis=0, tiled=True)  40.8 us
    dot_general x1, matrix products, expert_forward(): jnp.einsum('ecd,edf->ecf', expert_rows, w_up, preferred_element_type=jnp....  26.9 us
    dot_general x12, matrix products, head_forward(): jnp.einsum('ist,itd->isd', attn_probs, values_head, preferred_element_typ...  23.4 us
  transfers between devices with their start and end apart: 12, of which 9 were waited for; matrix products, arithmetic and copies ran while one was open for 31% of the time, Pallas kernels for 0%

commit v1 on v0

--- a/solution.py
+++ b/solution.py
@@ -9,6 +9,22 @@
 SEQ = 576
 CAP = 152
 norm_epsilon = 1e-06
+
+
+def ring_gather(x, axis, dim):
+    ways, here, step = (lax.axis_size(axis), lax.axis_index(axis), x.shape[dim])
+    dims = [n * ways if d == dim else n for d, n in enumerate(x.shape)]
+    full = lax.dynamic_update_slice_in_dim(jnp.zeros(dims, x.dtype), x, here * step, axis=dim)
+    going_up = going_down = x
+    for far in range(1, ways // 2 + 1):
+        going_up = lax.ppermute(going_up, axis, [(d, (d + 1) % ways) for d in range(ways)])
+        full = lax.dynamic_update_slice_in_dim(full, going_up, (here - far) % ways * step, axis=dim)
+        if 2 * far < ways:
+            going_down = lax.ppermute(going_down, axis, [(d, (d - 1) % ways) for d in range(ways)])
+            full = lax.dynamic_update_slice_in_dim(
+                full, going_down, (here + far) % ways * step, axis=dim
+            )
+    return full
 
 
 def norm_parts(values):
@@ -104,7 +120,7 @@
 def gather_experts(w_in, w_out):
     local_pair = (w_in, w_out)
     return (
-        lax.all_gather(local_pair[0], "fsdp", axis=1, tiled=True),
+        ring_gather(local_pair[0], "fsdp", 1),
         lax.all_gather(local_pair[1], "fsdp", axis=1, tiled=True),
     )
 

time: 1010 us -> 1090 us (1.079)
  starting transfers between devices: 18.3 us -> 100 us
  waiting for transfers between devices: 477 us -> 422 us
  local copies, waits for them, and re-layouts: 66.9 us -> 107 us
  blocking collectives: 126 us -> 146 us
    all_gather x1 -> x0, waiting for transfers between devices: 87.4 us -> none  [gather_experts(): lax.all_gather(local_pair[0], 'fsdp', axis=1, tiled=True)]
    ppermute x0 -> x15, starting transfers between devices: none -> 82.4 us  [the longest x8 71.8 us: ring_gather(): lax.ppermute(going_up, axis, [(d, (d + 1) % ways) for d in range(ways)])]
    ppermute x0 -> x15, waiting for transfers between devices: none -> 55.9 us  [the longest x8 55.9 us: ring_gather(): lax.ppermute(going_up, axis, [(d, (d + 1) % ways) for d in range(ways)])]
    dynamic_update_slice x0 -> x16, local copies, waits for them, and re-layouts: none -> 34.7 us  [the longest x8 18 us: ring_gather(): lax.dynamic_update_slice_in_dim(full, going_up, (here - far) % ways * ste...]
    unnamed x2, blocking collectives: 85.2 us -> 105 us
  transfers between devices with their start and end apart: 12 -> 26, of which waited for: 9 -> 10; matrix products, arithmetic and copies ran while one was open for 31% -> 31% of each run, Pallas kernels for 0% -> 0%
where the time goes in v1:
time: 1090 us
  waiting for transfers between devices  422 us (39%)
  matrix products  274 us (25%)
  blocking collectives  146 us (13%)
  local copies, waits for them, and re-layouts  107 us (10%)
  starting transfers between devices  100 us (9%)
  other arithmetic  22.5 us (2%)
  between operations  15.2 us (1%)
    reduce_scatter x1, waiting for transfers between devices, per_device(): lax.psum_scatter(d_qkv, ('dp', 'fsdp'), scatter_dimension=0, tiled=True)  125 us
    unnamed x2, blocking collectives  105 us
    reduce_scatter x1, waiting for transfers between devices, per_device(): lax.psum_scatter(d_proj, ('dp', 'fsdp'), scatter_dimension=0, tiled=True)  102 us
    reduce_scatter x1, waiting for transfers between devices, reduce_experts(): lax.psum_scatter(grad_down.astype(jnp.bfloat16), 'fsdp', scatter_dimensio...  88.8 us
    ppermute x8, starting transfers between devices, ring_gather(): lax.ppermute(going_up, axis, [(d, (d + 1) % ways) for d in range(ways)])  71.8 us
    ppermute x8, waiting for transfers between devices, ring_gather(): lax.ppermute(going_up, axis, [(d, (d + 1) % ways) for d in range(ways)])  55.9 us
    all_gather x1, blocking collectives, gather_dense(): lax.all_gather(w_router, ('dp', 'fsdp'), axis=0, tiled=True)  41.3 us
    dot_general x1, matrix products, expert_forward(): jnp.einsum('ecd,edf->ecf', expert_rows, w_up, preferred_element_type=jnp....  26.7 us
  transfers between devices with their start and end apart: 26, of which 10 were waited for; matrix products, arithmetic and copies ran while one was open for 31% of the time, Pallas kernels for 0%

profile of v1, /device:TPU:0, one launch (start us, length us, event | category | flops | bytes accessed | tf_op | source)
XLA Modules:
  0.0 1087.1 jit_solution(9432802819747360128)
XLA Ops:
  10.0 5.0 collective-permute-start.1
  15.0 14.8 %collective-permute-done = bf16[4,48,3072]{2,1,0:T(8,128)(2,1)S(1)} collective-permute-done((bf16[4,48,3072]{2,1,0:T(8,128)(2,1)}, bf16[4,48,3072]{2,1,0:T(8,128)(2,1)S(1)}, u32[]{:S(2)}, u32[]{:S(2)}) %collective-permute-start) | collective-permute-done | bytes 1179680 | tf_op jit(solution)/shard_map/ppermute | solution.py:20
  29.9 9.6 collective-permute-start.2
  39.7 9.8 collective-permute-done.2
  49.5 19.3 %collective-permute-start.4 = (bf16[4,48,3072]{2,1,0:T(8,128)(2,1)}, bf16[4,48,3072]{2,1,0:T(8,128)(2,1)}, u32[]{:S(2)}, u32[]{:S(2)}) collective-permute-start(bf16[4,48,3072]{2,1,0:T(8,128)(2,1)} %collective-permute-done.2), channel_id=1, source_target_pairs={{0,1},{1,2},{2,3},{3,4},{4,5},{5,6},{6,7},{7,8},{8,9},{9,10},{10,1... | collective-permute-start | bytes 3538952 | tf_op jit(solution)/shard_map/ppermute | solution.py:20
  69.9 6.8 broadcast.138
  77.8 24.9 %collective-permute-start.6 = (bf16[4,48,3072]{2,1,0:T(8,128)(2,1)}, bf16[4,48,3072]{2,1,0:T(8,128)(2,1)}, u32[]{:S(2)}, u32[]{:S(2)}) collective-permute-start(bf16[4,48,3072]{2,1,0:T(8,128)(2,1)} %collective-permute-done.4), channel_id=1, source_target_pairs={{0,1},{1,2},{2,3},{3,4},{4,5},{5,6},{6,7},{7,8},{8,9},{9,10},{10,1... | collective-permute-start | bytes 3538952 | tf_op jit(solution)/shard_map/ppermute | solution.py:20
  103.8 63.7 %all-reduce.6 = (bf16[768]{0:T(1024)(128)(2,1)S(1)}, bf16[768]{0:T(1024)(128)(2,1)S(1)}) all-reduce(bf16[768]{0:T(1024)(128)(2,1)S(1)} %dynamic-update-slice, bf16[768]{0:T(1024)(128)(2,1)S(1)} %dynamic-update-slice.1), channel_id=1, replica_groups=mesh['dp'=2,'fsdp'=16] {'dp','fsdp'}, use_global_device_ids=true, to_apply=%add | all-reduce | flops 1536 | bytes 6144
  167.5 41.3 %all-gather = bf16[32,24,8]{1,2,0:T(8,128)(2,1)S(1)} all-gather(bf16[1,24,8]{1,2,0:T(8,128)(2,1)S(1)} %bitcast.199), channel_id=1, replica_groups=mesh['dp'=2,'fsdp'=16] {'dp','fsdp'}, dimensions={0}, use_global_device_ids=true | all-gather | bytes 12672 | tf_op jit(solution)/shard_map/all_gather | solution.py:116
  209.0 2.5 constant_dynamic-update-slice_fusion.14
  213.8 2.4 constant_dynamic-update-slice_fusion.12
  216.6 4.1 collective-permute-start.9
  221.8 2.4 constant_dynamic-update-slice_fusion.10
  224.2 2.4 constant_dynamic-update-slice_fusion.9
  226.6 2.4 constant_dynamic-update-slice_fusion.8
  229.0 31.3 %collective-permute-done.8 = bf16[4,48,3072]{2,1,0:T(8,128)(2,1)} collective-permute-done((bf16[4,48,3072]{2,1,0:T(8,128)(2,1)}, bf16[4,48,3072]{2,1,0:T(8,128)(2,1)}, u32[]{:S(2)}, u32[]{:S(2)}) %collective-permute-start.8) | collective-permute-done | bytes 1179680 | tf_op jit(solution)/shard_map/ppermute | solution.py:20
  260.3 11.2 %collective-permute-start.10 = (bf16[4,48,3072]{2,1,0:T(8,128)(2,1)}, bf16[4,48,3072]{2,1,0:T(8,128)(2,1)}, u32[]{:S(2)}, u32[]{:S(2)}) collective-permute-start(bf16[4,48,3072]{2,1,0:T(8,128)(2,1)} %collective-permute-done.8), channel_id=1, source_target_pairs={{0,1},{1,2},{2,3},{3,4},{4,5},{5,6},{6,7},{7,8},{8,9},{9,10},{10,1... | collective-permute-start | bytes 3538952 | tf_op jit(solution)/shard_map/ppermute | solution.py:20
  271.7 5.9 convolution_convert_fusion.3
  277.6 4.0 copy.102
  287.2 2.6 copy.105
  289.8 37.7 %while.26 = (s32[]{:T(128)}, bf16[12,1,576,64]{2,3,1,0:T(8,128)(2,1)}, f32[12,1,576]{2,1,0:T(1,128)}, bf16[12,1,576,64]{3,2,1,0:T(8,128)(2,1)S(1)}, bf16[12,1,57...) while((s32[]{:T(128)}, bf16[12,1,576,64]{2,3,1,0:T(8,128)(2,1)}, ...), condition=%wide.region_5.6_spmd, body=%wide.region_2.5_spmd.sunk | while | flops 87293376 | bytes 4531033 | solution.py:153
  327.5 4.1 fusion.75
  333.3 3.7 fusion.48
  337.1 2.9 convolution_convert_fusion.4
  340.0 3.7 all-to-all-start.2
  343.7 3.1 collective-permute-start.12
  346.8 2.4 constant_dynamic-update-slice_fusion.7
  349.2 2.5 constant_dynamic-update-slice_fusion.6
  351.7 2.9 convolution_convert_fusion.5
  356.0 9.0 all-to-all-done.2
  366.2 4.8 all-to-all-start
  371.1 2.4 constant_dynamic-update-slice_fusion.5
  373.5 2.7 collective-permute-start.14
  376.2 2.4 constant_dynamic-update-slice_fusion.4
  378.6 2.5 constant_dynamic-update-slice_fusion.3
  381.2 12.4 %all-to-all-done = bf16[8,152,768]{2,1,0:T(8,128)(2,1)} async-done(((bf16[8,152,768]{2,1,0:T(8,128)(2,1)}), bf16[8,152,768]{2,1,0:T(8,128)(2,1)}, u32[]{:S(2)}, u32[]{:S(2)}) %all-to-all-start) | async-done | bytes 1867808 | tf_op jit(solution)/shard_map/all_to_all | solution.py:179
  393.6 2.9 copy.107
  398.8 2.4 constant_dynamic-update-slice_fusion.1
  402.4 12.9 %fusion.77 = f32[4,304,3072]{2,1,0:T(8,128)} fusion(bf16[4,304,768]{2,1,0:T(8,128)(2,1)S(1)} %bitcast.182, bf16[4,3072,768]{2,1,0:T(8,128)(2,1)} %all-gather.9.cloned.1.call-done), kind=kOutput, calls=%fused_computation.157 | convolution fusion | flops 5737807872 | bytes 35684352 | tf_op jit(solution)/shard_map/ecd,efd->ecf/dot_general | solution.py:97
  415.3 26.7 %fusion.43 = (bf16[4,304,3072]{2,1,0:T(8,128)(2,1)}, f32[4,304,3072]{2,1,0:T(8,128)}) fusion(f32[4,304,3072]{2,1,0:T(8,128)} %fusion.77, bf16[4,304,768]{2,1,0:T(8,128)(2,1)} %bitcast.192, bf16[4,768,3072]{2,1,0:T(8,128)(2,1)} %constant_dynamic-update-slice_fusion), kind=kOutput, calls=%fused_computation.59 | convolution fusion | flops 5812518912 | bytes 58097664 | tf_op jit(solution)/shard_map/ecd,edf->ecf/dot_general | solution.py:88
  442.0 16.5 %convolution_convert_fusion.2 = bf16[4,768,3072]{2,1,0:T(8,128)(2,1)} fusion(bf16[4,304,768]{2,1,0:T(8,128)(2,1)} %bitcast.193, bf16[4,304,3072]{2,1,0:T(8,128)(2,1)} %get-tuple-element.212), kind=kOutput, calls=%fused_computation.62 | convolution fusion | flops 5747245056 | bytes 28213248 | tf_op jit(solution)/shard_map/ecd,ecf->edf/dot_general | solution.py:103
  458.7 20.0 %convolution_convert_fusion.1 = bf16[4,3072,768]{2,1,0:T(8,128)(2,1)} fusion(bf16[4,304,768]{2,1,0:T(8,128)(2,1)S(1)} %bitcast.183, f32[4,304,3072]{2,1,0:T(8,128)} %get-tuple-element.213), kind=kOutput, calls=%fused_computation.61 | convolution fusion | flops 5780865024 | bytes 35684352 | tf_op jit(solution)/shard_map/ecf,ecd->efd/dot_general | solution.py:102
  478.8 19.1 %convolution_convert_fusion.7 = bf16[4,304,768]{2,1,0:T(8,128)(2,1)S(1)} fusion(bf16[4,3072,768]{2,1,0:T(8,128)(2,1)} %all-gather.9.cloned.1.call-done, f32[4,304,3072]{2,1,0:T(8,128)} %get-tuple-element.213), kind=kOutput, calls=%fused_computation.85 | convolution fusion | flops 5772361728 | bytes 35684352 | tf_op jit(solution)/shard_map/ecf,efd->ecd/dot_general | solution.py:90
  500.1 3.9 all-to-all-start.1
  504.0 13.2 %convolution_convert_fusion.6 = bf16[4,304,768]{2,1,0:T(8,128)(2,1)} fusion(bf16[4,304,3072]{2,1,0:T(8,128)(2,1)} %get-tuple-element.212, bf16[4,768,3072]{2,1,0:T(8,128)(2,1)} %constant_dynamic-update-slice_fusion), kind=kOutput, calls=%fused_computation.84 | convolution fusion | flops 5738741760 | bytes 28213248 | tf_op jit(solution)/shard_map/ecf,edf->ecd/dot_general | solution.py:104
  517.3 3.7 copy.112
  521.0 6.6 all-to-all-done.1
  528.9 4.7 all-to-all-start.3
  535.8 20.7 %all-to-all-done.3 = bf16[4,304,768]{2,0,1:T(4,128)(2,1)} async-done(((bf16[4,304,768]{2,0,1:T(4,128)(2,1)}), bf16[4,304,768]{2,0,1:T(4,128)(2,1)}, u32[]{:S(2)}, u32[]{:S(2)}) %all-to-all-start.3) | async-done | bytes 1867808 | tf_op jit(solution)/shard_map/all_to_all | solution.py:210
  559.6 4.8 gather_fusion
  564.4 4.7 reshape.217
  569.1 6.0 fusion.62
  576.4 3.1 fusion.78
  585.9 4.4 fusion.66
  590.6 100.8 %while.27 = (s32[]{:T(128)}, bf16[12,1,576,64]{2,3,1,0:T(8,128)(2,1)}, bf16[12,1,576,64]{2,3,1,0:T(8,128)(2,1)}, bf16[12,1,576,64]{2,3,1,0:T(8,128)(2,1)}, bf16[...) while((s32[]{:T(128)}, ...), condition=%wide.region_19.20_spmd, body=%wide.region_17.19_spmd.sunk | while | flops 215064000 | bytes 11510129 | solution.py:224
  695.3 5.5 fusion.71
  702.2 7.2 fusion.60
  709.3 41.1 %all-reduce.5 = (f32[768]{0:T(1024)S(1)}, f32[768]{0:T(1024)S(1)}, f32[768,8]{0,1:T(8,128)S(1)}) all-reduce(f32[768]{0:T(1024)S(1)} %get-tuple-element.158, f32[768]{0:T(1024)S(1)} %get-tuple-element.156, f32[768,8]{0,1:T(8,128)S(1)} %fusion.79), channel_id=2, replica_groups=mesh['dp'=2,'fsdp'=16] {'dp','fsdp'}, use_global_device_ids=true, to_apply=%region_23.24.clone | all-reduce | flops 7680 | bytes 61440
  752.3 4.1 fusion.59
  758.6 3.0 convert_element_type.122
  761.6 88.8 %reduce-scatter.12.cloned.1.call-done = bf16[4,192,768]{2,1,0:T(8,128)(2,1)} async-done(((bf16[4,3072,768]{2,1,0:T(8,128)(2,1)}), bf16[4,192,768]{2,1,0:T(8,128)(2,1)}) %reduce-scatter.12.cloned.1.call-update) | async-done | bytes 1179664 | tf_op jit(solution)/shard_map/reduce_scatter | solution.py:133
  850.4 2.9 convert_element_type.124
  853.2 101.7 %reduce-scatter.8.cloned.1.call-done = f32[24,768]{1,0:T(8,128)} async-done(((f32[768,768]{1,0:T(8,128)}), f32[24,768]{1,0:T(8,128)}) %reduce-scatter.8.cloned.1.call-update) | async-done | bytes 73744 | tf_op jit(solution)/shard_map/reduce_scatter | solution.py:242
  954.9 124.9 %reduce-scatter.6.cloned.1.call-done = f32[24,2304]{1,0:T(8,128)} async-done(((f32[768,2304]{1,0:T(8,128)}), f32[24,2304]{1,0:T(8,128)}) %reduce-scatter.6.cloned.1.call-update) | async-done | bytes 221200 | tf_op jit(solution)/shard_map/reduce_scatter | solution.py:241
  (330 shorter events, 188.2 us)
Async XLA Ops:
  7.2 32.3 %copy-start.8 = (bf16[576,768]{1,0:T(8,128)(2,1)S(1)}, bf16[576,768]{1,0:T(8,128)(2,1)}, u32[]{:S(2)}) copy-start(bf16[576,768]{1,0:T(8,128)(2,1)} %param.15) | copy-start | bytes 2654212
  7.2 62.0 %copy-start.26 = (s32[576,2]{0,1:T(2,128)S(1)}, s32[576,2]{0,1:T(2,128)}, u32[]{:S(2)}) copy-start(s32[576,2]{0,1:T(2,128)} %param.24) | copy-start | bytes 13828
  7.2 62.0 %copy-start.28 = (s32[576,2]{0,1:T(2,128)S(1)}, s32[576,2]{0,1:T(2,128)}, u32[]{:S(2)}) copy-start(s32[576,2]{0,1:T(2,128)} %param.23) | copy-start | bytes 13828
  7.2 264.5 %all-gather.5.cloned.1.call-start = ((), (), s32[]{:S(2)}) async-start(), calls=%async_computation.8 | async-start | bytes 3649536 | tf_op jit(solution)/shard_map/all_gather | solution.py:113
  7.9 319.6 %all-gather.7.cloned.1.call-start = ((), (), s32[]{:S(2)}) async-start(), calls=%async_computation.9 | async-start | bytes 1216512 | tf_op jit(solution)/shard_map/all_gather | solution.py:114
  8.7 393.7 %all-gather.9.cloned.1.call-start = ((), (), s32[]{:S(2)}) async-start(), calls=%async_computation.10 | async-start | bytes 20054016 | tf_op jit(solution)/shard_map/all_gather | solution.py:124
  9.4 20.4 %collective-permute-start = (bf16[4,48,3072]{2,1,0:T(8,128)(2,1)}, bf16[4,48,3072]{2,1,0:T(8,128)(2,1)S(1)}, u32[]{:S(2)}, u32[]{:S(2)}) collective-permute-start(bf16[4,48,3072]{2,1,0:T(8,128)(2,1)} %param.21), channel_id=1, source_target_pairs={{0,1},{1,2},{2,3},{3,4},{4,5},{5,6},{6,7},{7,8},{8,9},{9,10},{10,1... | collective-permute-start | bytes 3538952 | tf_op jit(solution)/shard_map/ppermute | solution.py:20
  10.0 29.5 %collective-permute-start.1 = (bf16[4,48,3072]{2,1,0:T(8,128)(2,1)}, bf16[4,48,3072]{2,1,0:T(8,128)(2,1)}, u32[]{:S(2)}, u32[]{:S(2)}) collective-permute-start(bf16[4,48,3072]{2,1,0:T(8,128)(2,1)} %param.21), channel_id=1, source_target_pairs={{0,15},{1,0},{2,1},{3,2},{4,3},{5,4},{6,5},{7,6},{8,7},{9,8},{10,9... | collective-permute-start | bytes 3538952 | tf_op jit(solution)/shard_map/ppermute | solution.py:23
  29.9 46.8 %copy-start.21 = (bf16[4,48,3072]{2,1,0:T(8,128)(2,1)}, bf16[4,48,3072]{2,1,0:T(8,128)(2,1)S(1)}, u32[]{:S(2)}) copy-start(bf16[4,48,3072]{2,1,0:T(8,128)(2,1)S(1)} %collective-permute-done) | copy-start | bytes 3538948
  29.9 19.6 %collective-permute-start.2 = (bf16[4,48,3072]{2,1,0:T(8,128)(2,1)S(1)}, bf16[4,48,3072]{2,1,0:T(8,128)(2,1)}, u32[]{:S(2)}, u32[]{:S(2)}) collective-permute-start(bf16[4,48,3072]{2,1,0:T(8,128)(2,1)S(1)} %collective-permute-done), channel_id=1, source_target_pairs={{0,1},{1,2},{2,3},{3,4},{4,5},{5,6},{6,7},{7,8},{8,9},{9,10},{10,1... | collective-permute-start | bytes 3538952 | tf_op jit(solution)/shard_map/ppermute | solution.py:20
  39.5 29.3 %collective-permute-start.3 = (bf16[4,48,3072]{2,1,0:T(8,128)(2,1)}, bf16[4,48,3072]{2,1,0:T(8,128)(2,1)S(1)}, u32[]{:S(2)}, u32[]{:S(2)}) collective-permute-start(bf16[4,48,3072]{2,1,0:T(8,128)(2,1)} %collective-permute-done.1), channel_id=1, source_target_pairs={{0,15},{1,0},{2,1},{3,2},{4,3},{5,4},{6,5},{7,6},{8,7},{9,8},{10,9... | collective-permute-start | bytes 3538952 | tf_op jit(solution)/shard_map/ppermute | solution.py:23
  49.5 28.4 %collective-permute-start.4 = (bf16[4,48,3072]{2,1,0:T(8,128)(2,1)}, bf16[4,48,3072]{2,1,0:T(8,128)(2,1)}, u32[]{:S(2)}, u32[]{:S(2)}) collective-permute-start(bf16[4,48,3072]{2,1,0:T(8,128)(2,1)} %collective-permute-done.2), channel_id=1, source_target_pairs={{0,1},{1,2},{2,3},{3,4},{4,5},{5,6},{6,7},{7,8},{8,9},{9,10},{10,1... | collective-permute-start | bytes 3538952 | tf_op jit(solution)/shard_map/ppermute | solution.py:20
  68.8 33.9 %collective-permute-start.5 = (bf16[4,48,3072]{2,1,0:T(8,128)(2,1)S(1)}, bf16[4,48,3072]{2,1,0:T(8,128)(2,1)}, u32[]{:S(2)}, u32[]{:S(2)}) collective-permute-start(bf16[4,48,3072]{2,1,0:T(8,128)(2,1)S(1)} %collective-permute-done.3), channel_id=1, source_target_pairs={{0,15},{1,0},{2,1},{3,2},{4,3},{5,4},{6,5},{7,6},{8,7},{9,8},{10,9... | collective-permute-start | bytes 3538952 | tf_op jit(solution)/shard_map/ppermute | solution.py:23
  68.8 202.9 %copy-start.30 = (f32[576]{0:T(1024)}, f32[576]{0:T(1024)S(1)}, u32[]{:S(2)}) copy-start(f32[576]{0:T(1024)S(1)} %broadcast_multiply_fusion.5) | copy-start | bytes 6916
  69.2 202.5 %copy-start.34 = (f32[576]{0:T(1024)}, f32[576]{0:T(1024)S(1)}, u32[]{:S(2)}) copy-start(f32[576]{0:T(1024)S(1)} %add_rsqrt_fusion.1) | copy-start | bytes 6916
  69.9 6.8 copy-start.19
  76.7 26.6 %copy-start.41 = (bf16[24]{0:T(256)(128)(2,1)S(1)}, bf16[24]{0:T(256)(128)(2,1)}, u32[]{:S(2)}) copy-start(bf16[24]{0:T(256)(128)(2,1)} %param.16) | copy-start | bytes 148
  76.7 26.9 %copy-start.42 = (bf16[24]{0:T(256)(128)(2,1)S(1)}, bf16[24]{0:T(256)(128)(2,1)}, u32[]{:S(2)}) copy-start(bf16[24]{0:T(256)(128)(2,1)} %param.19) | copy-start | bytes 148
  76.7 90.8 %copy-start.39 = (bf16[24,8]{0,1:T(8,128)(2,1)S(1)}, bf16[24,8]{0,1:T(8,128)(2,1)}, u32[]{:S(2)}) copy-start(bf16[24,8]{0,1:T(8,128)(2,1)} %param.20) | copy-start | bytes 1156
  77.8 138.4 %collective-permute-start.6 = (bf16[4,48,3072]{2,1,0:T(8,128)(2,1)}, bf16[4,48,3072]{2,1,0:T(8,128)(2,1)}, u32[]{:S(2)}, u32[]{:S(2)}) collective-permute-start(bf16[4,48,3072]{2,1,0:T(8,128)(2,1)} %collective-permute-done.4), channel_id=1, source_target_pairs={{0,1},{1,2},{2,3},{3,4},{4,5},{5,6},{6,7},{7,8},{8,9},{9,10},{10,1... | collective-permute-start | bytes 3538952 | tf_op jit(solution)/shard_map/ppermute | solution.py:20
  102.7 113.9 %collective-permute-start.7 = (bf16[4,48,3072]{2,1,0:T(8,128)(2,1)}, bf16[4,48,3072]{2,1,0:T(8,128)(2,1)S(1)}, u32[]{:S(2)}, u32[]{:S(2)}) collective-permute-start(bf16[4,48,3072]{2,1,0:T(8,128)(2,1)} %collective-permute-done.5), channel_id=1, source_target_pairs={{0,15},{1,0},{2,1},{3,2},{4,3},{5,4},{6,5},{7,6},{8,7},{9,8},{10,9... | collective-permute-start | bytes 3538952 | tf_op jit(solution)/shard_map/ppermute | solution.py:23
  167.5 104.2 %copy-start.36 = (f32[768]{0:T(1024)}, f32[768]{0:T(1024)S(1)}, u32[]{:S(2)}) copy-start(f32[768]{0:T(1024)S(1)} %convert_element_type.101) | copy-start | bytes 9220
  216.2 44.0 %collective-permute-start.8 = (bf16[4,48,3072]{2,1,0:T(8,128)(2,1)}, bf16[4,48,3072]{2,1,0:T(8,128)(2,1)}, u32[]{:S(2)}, u32[]{:S(2)}) collective-permute-start(bf16[4,48,3072]{2,1,0:T(8,128)(2,1)} %collective-permute-done.6), channel_id=1, source_target_pairs={{0,1},{1,2},{2,3},{3,4},{4,5},{5,6},{6,7},{7,8},{8,9},{9,10},{10,1... | collective-permute-start | bytes 3538952 | tf_op jit(solution)/shard_map/ppermute | solution.py:20
  216.6 7.6 copy-start.20
  216.6 54.8 %collective-permute-start.9 = (bf16[4,48,3072]{2,1,0:T(8,128)(2,1)S(1)}, bf16[4,48,3072]{2,1,0:T(8,128)(2,1)}, u32[]{:S(2)}, u32[]{:S(2)}) collective-permute-start(bf16[4,48,3072]{2,1,0:T(8,128)(2,1)S(1)} %collective-permute-done.7), channel_id=1, source_target_pairs={{0,15},{1,0},{2,1},{3,2},{4,3},{5,4},{6,5},{7,6},{8,7},{9,8},{10,9... | collective-permute-start | bytes 3538952 | tf_op jit(solution)/shard_map/ppermute | solution.py:23
  260.3 83.5 %collective-permute-start.10 = (bf16[4,48,3072]{2,1,0:T(8,128)(2,1)}, bf16[4,48,3072]{2,1,0:T(8,128)(2,1)}, u32[]{:S(2)}, u32[]{:S(2)}) collective-permute-start(bf16[4,48,3072]{2,1,0:T(8,128)(2,1)} %collective-permute-done.8), channel_id=1, source_target_pairs={{0,1},{1,2},{2,3},{3,4},{4,5},{5,6},{6,7},{7,8},{8,9},{9,10},{10,1... | collective-permute-start | bytes 3538952 | tf_op jit(solution)/shard_map/ppermute | solution.py:20
  271.5 83.2 %collective-permute-start.11 = (bf16[4,48,3072]{2,1,0:T(8,128)(2,1)}, bf16[4,48,3072]{2,1,0:T(8,128)(2,1)}, u32[]{:S(2)}, u32[]{:S(2)}) collective-permute-start(bf16[4,48,3072]{2,1,0:T(8,128)(2,1)} %collective-permute-done.9), channel_id=1, source_target_pairs={{0,15},{1,0},{2,1},{3,2},{4,3},{5,4},{6,5},{7,6},{8,7},{9,8},{10,9... | collective-permute-start | bytes 3538952 | tf_op jit(solution)/shard_map/ppermute | solution.py:23
  327.5 4.1 copy-start.4
  327.5 4.1 copy-start.5
  332.0 1.3 copy-start.29
  332.0 1.3 copy-start.32
  332.0 1.3 copy-start.38
  332.9 18.9 %copy-start.6 = (bf16[576,768]{1,0:T(8,128)(2,1)}, bf16[576,768]{1,0:T(8,128)(2,1)S(1)}, u32[]{:S(2)}) copy-start(bf16[576,768]{1,0:T(8,128)(2,1)S(1)} %multiply_convert_fusion.2) | copy-start | bytes 2654212
  332.9 4.2 copy-start.24
  337.1 2.9 copy-start.15
  340.0 25.0 %all-to-all-start.2 = ((bf16[8,152,768]{2,1,0:T(8,128)(2,1)}), bf16[8,152,768]{2,1,0:T(8,128)(2,1)S(1)}, u32[]{:S(2)}, u32[]{:S(2)}) async-start(bf16[8,152,768]{2,1,0:T(8,128)(2,1)} %bitcast.191), calls=%async_computation.2 | async-start | bytes 3735552 | tf_op jit(solution)/shard_map/all_to_all | solution.py:206
  343.7 29.8 %collective-permute-start.12 = (bf16[4,48,3072]{2,1,0:T(8,128)(2,1)}, bf16[4,48,3072]{2,1,0:T(8,128)(2,1)}, u32[]{:S(2)}, u32[]{:S(2)}) collective-permute-start(bf16[4,48,3072]{2,1,0:T(8,128)(2,1)} %collective-permute-done.10), channel_id=1, source_target_pairs={{0,1},{1,2},{2,3},{3,4},{4,5},{5,6},{6,7},{7,8},{8,9},{9,10},{10,1... | collective-permute-start | bytes 3538952 | tf_op jit(solution)/shard_map/ppermute | solution.py:20
  349.2 2.5 copy-start.17
  354.6 44.2 %collective-permute-start.13 = (bf16[4,48,3072]{2,1,0:T(8,128)(2,1)}, bf16[4,48,3072]{2,1,0:T(8,128)(2,1)}, u32[]{:S(2)}, u32[]{:S(2)}) collective-permute-start(bf16[4,48,3072]{2,1,0:T(8,128)(2,1)} %collective-permute-done.11), channel_id=1, source_target_pairs={{0,15},{1,0},{2,1},{3,2},{4,3},{5,4},{6,5},{7,6},{8,7},{9,8},{10,9... | collective-permute-start | bytes 3538952 | tf_op jit(solution)/shard_map/ppermute | solution.py:23
  365.0 1.2 copy-start.11
  366.2 27.4 %all-to-all-start = ((bf16[8,152,768]{2,1,0:T(8,128)(2,1)}), bf16[8,152,768]{2,1,0:T(8,128)(2,1)}, u32[]{:S(2)}, u32[]{:S(2)}) async-start(bf16[8,152,768]{2,1,0:T(8,128)(2,1)} %bitcast.190), calls=%async_computation | async-start | bytes 3735552 | tf_op jit(solution)/shard_map/all_to_all | solution.py:179
  371.1 387.6 %reduce-scatter.10.cloned.1.call-start = ((), (), s32[]{:S(2)}) async-start(), calls=%async_computation.13 | async-start | bytes 20054016 | tf_op jit(solution)/shard_map/reduce_scatter | solution.py:130
  373.5 27.8 %collective-permute-start.14 = (bf16[4,48,3072]{2,1,0:T(8,128)(2,1)}, bf16[4,48,3072]{2,1,0:T(8,128)(2,1)S(1)}, u32[]{:S(2)}, u32[]{:S(2)}) collective-permute-start(bf16[4,48,3072]{2,1,0:T(8,128)(2,1)} %collective-permute-done.12), channel_id=1, source_target_pairs={{0,1},{1,2},{2,3},{3,4},{4,5},{5,6},{6,7},{7,8},{8,9},{9,10},{10,1... | collective-permute-start | bytes 3538952 | tf_op jit(solution)/shard_map/ppermute | solution.py:20
  378.6 2.5 copy-start.12
  458.5 391.9 %reduce-scatter.12.cloned.1.call-start = ((), (), s32[]{:S(2)}) async-start(), calls=%async_computation.14 | async-start | bytes 20054016 | tf_op jit(solution)/shard_map/reduce_scatter | solution.py:133
  500.1 27.5 %all-to-all-start.1 = ((bf16[4,304,768]{2,0,1:T(4,128)(2,1)}), bf16[4,304,768]{2,0,1:T(4,128)(2,1)S(1)}, u32[]{:S(2)}, u32[]{:S(2)}) async-start(bf16[4,304,768]{2,0,1:T(4,128)(2,1)} %copy.108), calls=%async_computation.1 | async-start | bytes 3735552 | tf_op jit(solution)/shard_map/all_to_all | solution.py:181
  521.0 12.7 %copy-start.33 = (s32[576,2]{0,1:T(2,128)S(1)}, s32[576,2]{0,1:T(2,128)}, u32[]{:S(2)}) copy-start(s32[576,2]{0,1:T(2,128)} %get-tuple-element.199) | copy-start | bytes 13828
  528.9 27.7 %all-to-all-start.3 = ((bf16[4,304,768]{2,0,1:T(4,128)(2,1)}), bf16[4,304,768]{2,0,1:T(4,128)(2,1)}, u32[]{:S(2)}, u32[]{:S(2)}) async-start(bf16[4,304,768]{2,0,1:T(4,128)(2,1)} %copy.112), calls=%async_computation.3 | async-start | bytes 3735552 | tf_op jit(solution)/shard_map/all_to_all | solution.py:210
  533.6 421.3 %reduce-scatter.8.cloned.1.call-start = ((), (), s32[]{:S(2)}) async-start(), calls=%async_computation.12 | async-start | bytes 2433024 | tf_op jit(solution)/shard_map/reduce_scatter | solution.py:242
  569.1 7.1 copy-start.27
  569.1 7.2 copy-start.18
  576.4 3.1 copy-start.1
  580.6 1.9 copy-start.40
  590.3 489.5 %reduce-scatter.6.cloned.1.call-start = ((), (), s32[]{:S(2)}) async-start(), calls=%async_computation.11 | async-start | bytes 7299072 | tf_op jit(solution)/shard_map/reduce_scatter | solution.py:241
  691.4 1.5 copy-start.22
  691.4 1.8 copy-start.23
  693.1 2.2 copy-start.9
  693.2 2.2 copy-start.31
  693.2 2.2 copy-start.35
  693.2 2.2 copy-start.37
  693.7 1.6 copy-start.14
  702.2 50.1 %copy-start.10 = (bf16[576,768]{1,0:T(8,128)(2,1)S(1)}, bf16[576,768]{1,0:T(8,128)(2,1)}, u32[]{:S(2)}) copy-start(bf16[576,768]{1,0:T(8,128)(2,1)} %param.15) | copy-start | bytes 2654212
  752.3 4.1 copy-start.2
  752.3 4.1 copy-start.16
  (5 other events, 6.0 us)
Sparse Core Ops, SparseCore 0:
  10.9 86.0 all-gather.4
  100.0 60.7 all-gather.6
  162.4 141.8 all-gather.8
  458.6 193.5 reduce-scatter.9
  656.2 194.1 reduce-scatter.11
  856.1 98.7 reduce-scatter.7
  961.2 118.5 reduce-scatter.5
